TPU v7x, 128 devices: a whole 4x4x4 slice. The times are simulated.
128 devices in a mesh: replica: 8 (over x, y_hi), shard: 16 (over z, y_lo, core).
Axes of the slice: x: 4, y: 4 (y_hi: 2, y_lo: 2; y = y_hi * 2 + y_lo), z: 4, core: 2. Of those that a mesh axis runs over, the one named last changes fastest.
Arguments:
- tokens: bfloat16 [65536, 1920], P(('replica', 'shard')), may hold values from -36 to 36
- timesteps: int32 [256], P(('replica', 'shard')), may hold values from 0 to 63
- table: float32 [64, 2, 1920], replicated, may hold values from -3 to 3
- weight_values: bfloat16 [4864, 1920], P('shard'), may hold values from -0.125 to 0.125
- weight_scales: bfloat16 [4864, 15], P('shard'), may hold values from 0.29882812 to 3
- cotangent: bfloat16 [65536, 4864], P(('replica', 'shard')), may hold values from -24 to 24
Outputs:
- hidden: bfloat16 [65536, 4864], P(('replica', 'shard'))
- grad_weight: float32 [4864, 1920], P('shard')
- grad_tokens: bfloat16 [65536, 1920], P(('replica', 'shard'))
All inputs are finite; a program needn't handle non-finite values.
Results may differ from a plain program's by a relative error of at most 0.02.
Values may be sent and summed in bfloat16 or wider, within the bound.
A program may use at most 256 MiB of HBM per device.

v0:
```python
import jax
import jax.numpy as jnp
from jax import lax
from jax.sharding import PartitionSpec as P

root_two_over_pi = 0.7978845608028654
cubic_coef = 0.044715
epsilon = 1e-06


def gelu_slope(preact):
    inner_term = root_two_over_pi * (preact + cubic_coef * preact * preact * preact)
    tangent = jnp.tanh(inner_term)
    gelu_value = 0.5 * preact * (1.0 + tangent)
    derivative = 0.5 * (1.0 + tangent) + 0.5 * preact * (
        1.0 - tangent * tangent
    ) * root_two_over_pi * (1.0 + 3.0 * cubic_coef * preact * preact)
    return (gelu_value, derivative)


def dequantize(weight_values, weight_scales):
    row_count, features = weight_values.shape
    blocks = weight_scales.shape[1]
    expanded = (
        weight_values.astype(jnp.float32).reshape(row_count, blocks, features // blocks)
        * weight_scales.astype(jnp.float32)[:, :, None]
    )
    return expanded.reshape(row_count, features).astype(jnp.bfloat16)


def modulate(tokens, timesteps, table):
    samples = timesteps.shape[0]
    step_count = table.shape[0]
    features = tokens.shape[1]
    onehot = (timesteps[:, None] == jnp.arange(step_count, dtype=jnp.int32)[None, :]).astype(
        jnp.float32
    )
    picked = jnp.dot(
        onehot, table.reshape(step_count, 2 * features), precision=lax.Precision.HIGHEST
    )
    picked = picked.reshape(samples, 2, features)
    grouped = tokens.astype(jnp.float32).reshape(samples, -1, features)
    centre = grouped - jnp.mean(grouped, axis=2, keepdims=True)
    inverse = lax.rsqrt(jnp.mean(centre * centre, axis=2, keepdims=True) + epsilon)
    normed = centre * inverse
    factor = 1.0 + picked[:, 1][:, None, :]
    moved = (normed * factor + picked[:, 0][:, None, :]).reshape(-1, features).astype(jnp.bfloat16)
    return (moved, normed, inverse, factor)


def normalize_back(grad_moved, normed, inverse, factor):
    samples = normed.shape[0]
    features = normed.shape[2]
    scaled_grad = grad_moved.reshape(samples, -1, features) * factor
    mean_grad = jnp.mean(scaled_grad, axis=2, keepdims=True)
    mean_prod = jnp.mean(scaled_grad * normed, axis=2, keepdims=True)
    result = inverse * (scaled_grad - mean_grad - normed * mean_prod)
    return result.reshape(-1, features).astype(jnp.bfloat16)


def per_device(tokens, timesteps, table, weight_values, weight_scales, cotangent):
    moved, normed, inverse, factor = modulate(tokens, timesteps, table)
    upstream = cotangent.astype(jnp.float32)
    weight = lax.all_gather(dequantize(weight_values, weight_scales), "shard", axis=0, tiled=True)
    preact = jnp.einsum("td,fd->tf", moved, weight, preferred_element_type=jnp.float32)
    gelu_value, derivative = gelu_slope(preact)
    hidden = gelu_value.astype(jnp.bfloat16)
    grad_pre = (upstream * derivative).astype(jnp.bfloat16)
    grad_moved = jnp.dot(grad_pre, weight, preferred_element_type=jnp.float32)
    product = lax.dot_general(
        grad_pre, moved, (((0,), (0,)), ((), ())), preferred_element_type=jnp.float32
    )
    rounded = lax.optimization_barrier(product.astype(jnp.bfloat16))
    group_part = lax.psum_scatter(
        rounded.astype(jnp.float32).astype(jnp.bfloat16), "shard", scatter_dimension=0, tiled=True
    )
    grad_weight = lax.psum(group_part, "replica").astype(jnp.float32)
    grad_tokens = normalize_back(grad_moved, normed, inverse, factor)
    return (hidden, grad_weight, grad_tokens)


def solution(mesh):
    placed = (
        P(("replica", "shard"), None),
        P(("replica", "shard")),
        P(),
        P("shard", None),
        P("shard", None),
        P(("replica", "shard"), None),
    )
    return jax.shard_map(
        per_device,
        mesh=mesh,
        in_specs=placed,
        out_specs=(P(("replica", "shard"), None), P("shard", None), P(("replica", "shard"), None)),
        check_vma=False,
    )
```

profile of v0, /device:TPU:0, one launch (start us, length us, event | category | flops | bytes accessed | tf_op | source)
XLA Modules:
  0.0 461.4 jit_solution(8686879250005387591)
XLA Ops:
  7.2 0.0 copy-start
  7.2 0.0 copy-start.1
  7.2 0.0 copy-start.2
  7.2 0.0 all-gather.2.cloned.1.call-start
  7.2 1.0 copy.11
  8.2 0.7 mul.124
  8.9 3.1 fusion.18
  12.0 0.0 all-gather.2.cloned.1.call-update
  12.0 0.0 reduce-scatter.2.cloned.1.call-start
  12.1 0.0 copy-done
  12.1 0.3 convert_reduce_fusion
  12.4 0.7 fusion.15
  13.1 0.0 copy-done.1
  13.1 0.0 copy-done.2
  13.1 0.4 fusion.19
  13.6 2.5 fusion.17
  16.1 99.2 %all-gather.2.cloned.1.call-done = bf16[4864,1920]{1,0:T(8,128)(2,1)} async-done(((bf16[304,1920]{1,0:T(8,128)(2,1)}), bf16[4864,1920]{1,0:T(8,128)(2,1)}) %all-gather.2.cloned.1.call-update) | async-done | bytes 18677776 | tf_op jit(solution)/shard_map/all_gather | solution.py:64
  115.3 18.7 %multiply_convert_fusion = (bf16[512,4864]{1,0:T(8,128)(2,1)}, f32[512,4864]{1,0:T(8,128)}) fusion(bf16[512,1920]{1,0:T(8,128)(2,1)} %fusion.17, bf16[4864,1920]{1,0:T(8,128)(2,1)} %all-gather.2.cloned.1.call-done), kind=kOutput, calls=%fused_computation.10 | convolution fusion | flops 9585426432 | bytes 35586048 | tf_op jit(solution)/shard_map/td,fd->tf/dot_general | solution.py:65
  134.0 23.2 %convolution_convert_fusion = bf16[4864,1920]{1,0:T(8,128)(2,1)} fusion(bf16[512,1920]{1,0:T(8,128)(2,1)} %fusion.17, f32[512,4864]{1,0:T(8,128)} %get-tuple-element.8, bf16[512,4864]{1,0:T(8,128)(2,1)} %param.11), kind=kOutput, calls=%fused_computation | convolution fusion | flops 9622159360 | bytes 35586048 | tf_op jit(solution)/shard_map/dot_general | solution.py:70
  157.2 0.0 reduce-scatter.2.cloned.1.call-update
  157.2 0.0 all-reduce.2.cloned.1.call-start
  157.3 203.4 %reduce-scatter.2.cloned.1.call-done = bf16[304,1920]{1,0:T(8,128)(2,1)} async-done(((bf16[4864,1920]{1,0:T(8,128)(2,1)}), bf16[304,1920]{1,0:T(8,128)(2,1)}) %reduce-scatter.2.cloned.1.call-update) | async-done | bytes 1167376 | tf_op jit(solution)/shard_map/reduce_scatter | solution.py:74
  360.7 0.0 all-reduce.2.cloned.1.call-update
  360.7 23.9 %fusion.29 = (f32[512]{0:T(512)S(1)}, f32[512]{0:T(512)S(1)}, f32[512,1920]{1,0:T(8,128)S(1)}) fusion(f32[512]{0:T(512)S(1)} %add_rsqrt_fusion, f32[512]{0:T(512)S(1)} %broadcast_multiply_fusion.2, bf16[512,1920]{1,0:T(8,128)(2,1)S(1)} %copy-done, f32[2,1920]{1,0:T(2,128)S(1)} %get-tuple-element.5, bf16[4864,1920]{1,0:T(8,128)(2,1)} %all-gather.2.cloned.1.call-done, ...), kind=kOutput, calls=%fused_computation.42 | convolution fusion | flops 9619701760 | bytes 39541760 | tf_op jit(solution)/shard_map/dot_general | solution.py:69
  384.6 2.4 fusion.14
  387.0 65.1 %all-reduce.2.cloned.1.call-done = bf16[304,1920]{1,0:T(8,128)(2,1)} async-done(((bf16[304,1920]{1,0:T(8,128)(2,1)}), bf16[304,1920]{1,0:T(8,128)(2,1)}) %all-reduce.2.cloned.1.call-update) | async-done | bytes 1167376 | tf_op jit(solution)/shard_map/psum | solution.py:77
  452.1 2.8 convert_element_type.45
  (4 shorter events, 0.0 us)
Async XLA Ops:
  7.2 4.9 %copy-start = (bf16[512,1920]{1,0:T(8,128)(2,1)S(1)}, bf16[512,1920]{1,0:T(8,128)(2,1)}, u32[]{:S(2)}) copy-start(bf16[512,1920]{1,0:T(8,128)(2,1)} %param.6) | copy-start | bytes 5898244
  7.2 5.9 %copy-start.1 = (f32[64,2,1920]{2,1,0:T(2,128)S(1)}, f32[64,2,1920]{2,1,0:T(2,128)}, u32[]{:S(2)}) copy-start(f32[64,2,1920]{2,1,0:T(2,128)} %param.8) | copy-start | bytes 2949124
  7.2 5.9 %copy-start.2 = (s32[2]{0:T(128)S(1)}, s32[2]{0:T(128)}, u32[]{:S(2)}) copy-start(s32[2]{0:T(128)} %param.7) | copy-start | bytes 28
  7.2 108.1 %all-gather.2.cloned.1.call-start = ((), (), s32[]{:S(2)}) async-start(), calls=%async_computation.1 | async-start | bytes 19845120 | tf_op jit(solution)/shard_map/all_gather | solution.py:64
  12.0 348.6 %reduce-scatter.2.cloned.1.call-start = ((), (), s32[]{:S(2)}) async-start(), calls=%async_computation.2 | async-start | bytes 19845120 | tf_op jit(solution)/shard_map/reduce_scatter | solution.py:74
  157.2 294.8 %all-reduce.2.cloned.1.call-start = ((), (), s32[]{:S(2)}) async-start(), calls=%async_computation.3 | async-start | bytes 2334720 | tf_op jit(solution)/shard_map/psum | solution.py:77
Sparse Core Ops, SparseCore 0:
  12.2 103.0 all-gather.1
  157.4 203.2 reduce-scatter.1
  363.4 88.6 all-reduce.1
where the time goes:
time: 462 us; the launch traced here: 461 us
  waiting for transfers between devices  368 us (80%)
  matrix products  66.3 us (14%)
  between operations  13.8 us (3%)
  other arithmetic  11.8 us (3%)
    reduce_scatter x1, waiting for transfers between devices, per_device(): lax.psum_scatter(rounded.astype(jnp.float32).astype(jnp.bfloat16), 'shard...  203 us
    all_gather x1, waiting for transfers between devices, per_device(): lax.all_gather(dequantize(weight_values, weight_scales), 'shard', axis=0,...  99.2 us
    psum x1, waiting for transfers between devices, per_device(): grad_weight = lax.psum(group_part, 'replica').astype(jnp.float32)  65.1 us
    dot_general x1, matrix products, per_device(): grad_moved = jnp.dot(grad_pre, weight, preferred_element_type=jnp.float32)  23.9 us
    dot_general x1, matrix products, per_device(): lax.dot_general(grad_pre, moved, (((0,), (0,)), ((), ())), preferred_elem...  23.2 us
    dot_general x1, matrix products, per_device(): jnp.einsum('td,fd->tf', moved, weight, preferred_element_type=jnp.float32)  18.7 us
  transfers between devices with their start and end apart: 3, of which 3 were waited for; matrix products, arithmetic and copies ran while one was open for 7% of the time, Pallas kernels for 0%

commit v1 on v0

--- a/solution.py
+++ b/solution.py
@@ -61,7 +61,15 @@
 def per_device(tokens, timesteps, table, weight_values, weight_scales, cotangent):
     moved, normed, inverse, factor = modulate(tokens, timesteps, table)
     upstream = cotangent.astype(jnp.float32)
-    weight = lax.all_gather(dequantize(weight_values, weight_scales), "shard", axis=0, tiled=True)
+    weight = jnp.concatenate(
+        lax.all_to_all(
+            jnp.stack([dequantize(weight_values, weight_scales)] * lax.axis_size("shard")),
+            "shard",
+            0,
+            0,
+        ),
+        axis=0,
+    )
     preact = jnp.einsum("td,fd->tf", moved, weight, preferred_element_type=jnp.float32)
     gelu_value, derivative = gelu_slope(preact)
     hidden = gelu_value.astype(jnp.bfloat16)

time: 462 us -> 572 us (1.24)
  waiting for transfers between devices: 368 us -> 476 us
  matrix products: 66.3 us -> 56 us
  starting transfers between devices: 0.12 us -> 6.77 us
  local copies, waits for them, and re-layouts: 1.69 us -> 8.31 us
    all_to_all x0 -> x1, waiting for transfers between devices: none -> 201 us  [per_device(): lax.all_to_all(jnp.stack([dequantize(weight_values, weight_scales)] * lax...]
    all_gather x1 -> x0, waiting for transfers between devices: 99.2 us -> none  [per_device(): lax.all_gather(dequantize(weight_values, weight_scales), 'shard', axis=0,...]
    dot_general x1, matrix products: 23.9 us -> 16.2 us  [per_device(): grad_moved = jnp.dot(grad_pre, weight, preferred_element_type=jnp.float32)]
    psum x1, waiting for transfers between devices: 65.1 us -> 72.6 us  [per_device(): grad_weight = lax.psum(group_part, 'replica').astype(jnp.float32)]
    all_to_all x0 -> x1, starting transfers between devices: none -> 6.69 us  [per_device(): lax.all_to_all(jnp.stack([dequantize(weight_values, weight_scales)] * lax...]
    another operation x0 -> x1, local copies, waits for them, and re-layouts: none -> 6.62 us  [per_device(): jnp.stack([dequantize(weight_values, weight_scales)] * lax.axis_size('sha...]
    dot_general x1, matrix products: 23.2 us -> 16.6 us  [per_device(): lax.dot_general(grad_pre, moved, (((0,), (0,)), ((), ())), preferred_elem...]
  transfers between devices with their start and end apart: 3 -> 3, of which waited for: 3 -> 3; matrix products, arithmetic and copies ran while one was open for 7% -> 4% of each run, Pallas kernels for 0% -> 0%
where the time goes in v1:
time: 572 us
  waiting for transfers between devices  476 us (83%)
  matrix products  56 us (10%)
  between operations  14.1 us (2%)
  other arithmetic  10.8 us (2%)
  local copies, waits for them, and re-layouts  8.31 us (1%)
  starting transfers between devices  6.77 us (1%)
    reduce_scatter x1, waiting for transfers between devices, per_device(): lax.psum_scatter(rounded.astype(jnp.float32).astype(jnp.bfloat16), 'shard...  202 us
    all_to_all x1, waiting for transfers between devices, per_device(): lax.all_to_all(jnp.stack([dequantize(weight_values, weight_scales)] * lax...  201 us
    psum x1, waiting for transfers between devices, per_device(): grad_weight = lax.psum(group_part, 'replica').astype(jnp.float32)  72.6 us
    dot_general x1, matrix products, per_device(): jnp.einsum('td,fd->tf', moved, weight, preferred_element_type=jnp.float32)  22.7 us
    dot_general x1, matrix products, per_device(): lax.dot_general(grad_pre, moved, (((0,), (0,)), ((), ())), preferred_elem...  16.6 us
    dot_general x1, matrix products, per_device(): grad_moved = jnp.dot(grad_pre, weight, preferred_element_type=jnp.float32)  16.2 us
  transfers between devices with their start and end apart: 3, of which 3 were waited for; matrix products, arithmetic and copies ran while one was open for 4% of the time, Pallas kernels for 0%

profile of v1, /device:TPU:0, one launch (start us, length us, event | category | flops | bytes accessed | tf_op | source)
XLA Modules:
  0.0 572.0 jit_solution(15016844571071779987)
XLA Ops:
  7.2 0.8 copy.11
  8.0 0.7 mul.120
  8.7 2.1 fusion.8
  10.8 6.6 %stack.2 = bf16[16,304,1920]{2,1,0:T(8,128)(2,1)} broadcast(bf16[304,1920]{1,0:T(8,128)(2,1)S(1)} %fusion.8), dimensions={1,2} | broadcast | bytes 19845120 | tf_op jit(solution)/shard_map/stack | solution.py:66
  17.4 0.0 copy-start
  17.4 6.7 %all-to-all-start = ((bf16[16,304,1920]{2,1,0:T(8,128)(2,1)}), bf16[16,304,1920]{2,1,0:T(8,128)(2,1)}, u32[]{:S(2)}, u32[]{:S(2)}) async-start(bf16[16,304,1920]{2,1,0:T(8,128)(2,1)} %stack.2), calls=%async_computation | async-start | bytes 37355520 | tf_op jit(solution)/shard_map/all_to_all | solution.py:65
  24.1 0.0 copy-start.1
  24.1 0.0 copy-start.2
  24.1 0.0 reduce-scatter.2.cloned.1.call-start
  24.2 0.0 copy-done
  24.2 0.3 convert_reduce_fusion
  24.5 0.7 multiply_reduce_fusion.1
  25.2 0.1 copy-done.1
  25.3 0.0 copy-done.2
  25.3 0.4 fusion.9
  25.8 2.5 fusion.7
  28.2 201.5 %all-to-all-done = bf16[16,304,1920]{2,1,0:T(8,128)(2,1)} async-done(((bf16[16,304,1920]{2,1,0:T(8,128)(2,1)}), bf16[16,304,1920]{2,1,0:T(8,128)(2,1)}, u32[]{:S(2)}, u32[]{:S(2)}) %all-to-all-start) | async-done | bytes 18677792 | tf_op jit(solution)/shard_map/all_to_all | solution.py:65
  229.7 22.7 %fusion.6 = (bf16[512,4864]{1,0:T(8,128)(2,1)}, bf16[512,4864]{1,0:T(8,128)(2,1)}) fusion(bf16[512,4864]{1,0:T(8,128)(2,1)} %param.11, bf16[512,1920]{1,0:T(8,128)(2,1)} %fusion.7, bf16[4864,1920]{1,0:T(8,128)(2,1)} %bitcast.6), kind=kOutput, calls=%fused_computation.9 | convolution fusion | flops 9617801216 | bytes 35586048 | tf_op jit(solution)/shard_map/td,fd->tf/dot_general | solution.py:73
  252.4 16.6 %convolution_convert_fusion = bf16[4864,1920]{1,0:T(8,128)(2,1)} fusion(bf16[512,4864]{1,0:T(8,128)(2,1)} %get-tuple-element.5, bf16[512,1920]{1,0:T(8,128)(2,1)} %fusion.7), kind=kOutput, calls=%fused_computation | convolution fusion | flops 9572352000 | bytes 25624576 | tf_op jit(solution)/shard_map/dot_general | solution.py:78
  269.1 0.0 reduce-scatter.2.cloned.1.call-update
  269.1 0.0 all-reduce.2.cloned.1.call-start
  269.2 202.0 %reduce-scatter.2.cloned.1.call-done = bf16[304,1920]{1,0:T(8,128)(2,1)} async-done(((bf16[4864,1920]{1,0:T(8,128)(2,1)}), bf16[304,1920]{1,0:T(8,128)(2,1)}) %reduce-scatter.2.cloned.1.call-update) | async-done | bytes 1167376 | tf_op jit(solution)/shard_map/reduce_scatter | solution.py:82
  471.1 0.0 all-reduce.2.cloned.1.call-update
  471.2 16.2 %fusion.17 = (f32[2,256]{1,0:T(2,128)S(1)}, f32[2,256]{1,0:T(2,128)S(1)}, f32[2,256,1920]{2,1,0:T(8,128)S(1)}) fusion(f32[2,256]{1,0:T(2,128)S(1)} %rsqrt.13, f32[2,256]{1,0:T(2,128)S(1)} %div.17, f32[2,1920]{1,0:T(2,128)S(1)} %get-tuple-element.7, bf16[2,256,4864]{2,1,0:T(8,128)(2,1)} %bitcast.49, bf16[4864,1920,1]{1,0,2:T(8,128)(2,1)} %bitcast.8, ...), kind=kOutput, calls=%fused_computation.36 | convolution fusion | flops 9569894400 | bytes 29580288 | tf_op jit(solution)/shard_map/dot_general | solution.py:77
  487.4 2.4 multiply_convert_fusion.1
  489.8 72.6 %all-reduce.2.cloned.1.call-done = bf16[304,1920]{1,0:T(8,128)(2,1)} async-done(((bf16[304,1920]{1,0:T(8,128)(2,1)}), bf16[304,1920]{1,0:T(8,128)(2,1)}) %all-reduce.2.cloned.1.call-update) | async-done | bytes 1167376 | tf_op jit(solution)/shard_map/psum | solution.py:85
  562.3 2.8 convert_element_type.48
  (6 shorter events, 0.1 us)
Async XLA Ops:
  17.4 6.8 %copy-start = (bf16[512,1920]{1,0:T(8,128)(2,1)S(1)}, bf16[512,1920]{1,0:T(8,128)(2,1)}, u32[]{:S(2)}) copy-start(bf16[512,1920]{1,0:T(8,128)(2,1)} %param.6) | copy-start | bytes 5898244
  17.4 212.3 %all-to-all-start = ((bf16[16,304,1920]{2,1,0:T(8,128)(2,1)}), bf16[16,304,1920]{2,1,0:T(8,128)(2,1)}, u32[]{:S(2)}, u32[]{:S(2)}) async-start(bf16[16,304,1920]{2,1,0:T(8,128)(2,1)} %stack.2), calls=%async_computation | async-start | bytes 37355520 | tf_op jit(solution)/shard_map/all_to_all | solution.py:65
  24.1 1.2 copy-start.1
  24.1 1.2 copy-start.2
  24.1 447.0 %reduce-scatter.2.cloned.1.call-start = ((), (), s32[]{:S(2)}) async-start(), calls=%async_computation.2 | async-start | bytes 19845120 | tf_op jit(solution)/shard_map/reduce_scatter | solution.py:82
  269.1 293.2 %all-reduce.2.cloned.1.call-start = ((), (), s32[]{:S(2)}) async-start(), calls=%async_computation.3 | async-start | bytes 2334720 | tf_op jit(solution)/shard_map/psum | solution.py:85
Sparse Core Ops, SparseCore 0:
  269.2 201.8 reduce-scatter.1
  473.8 88.4 all-reduce.1

commit v2 on v0

--- a/solution.py
+++ b/solution.py
@@ -74,7 +74,7 @@
     group_part = lax.psum_scatter(
         rounded.astype(jnp.float32).astype(jnp.bfloat16), "shard", scatter_dimension=0, tiled=True
     )
-    grad_weight = lax.psum(group_part, "replica").astype(jnp.float32)
+    grad_weight = jnp.sum(lax.all_gather(group_part, "replica"), axis=0).astype(jnp.float32)
     grad_tokens = normalize_back(grad_moved, normed, inverse, factor)
     return (hidden, grad_weight, grad_tokens)
 

time: 462 us -> 494 us (1.069)
  waiting for transfers between devices: 368 us -> 395 us
    all_gather x0 -> x1, waiting for transfers between devices: none -> 92.5 us  [per_device(): lax.all_gather(group_part, 'replica')]
    psum x1 -> x0, waiting for transfers between devices: 65.1 us -> none  [per_device(): grad_weight = lax.psum(group_part, 'replica').astype(jnp.float32)]
    reduce_sum x0 -> x1, other arithmetic: none -> 5.56 us  [per_device(): jnp.sum(lax.all_gather(group_part, 'replica'), axis=0).astype(jnp.float32)]
  transfers between devices with their start and end apart: 3 -> 3, of which waited for: 3 -> 3; matrix products, arithmetic and copies ran while one was open for 7% -> 6% of each run, Pallas kernels for 0% -> 0%
where the time goes in v2:
time: 494 us; the launch traced here: 493 us
  waiting for transfers between devices  395 us (80%)
  matrix products  66.3 us (13%)
  other arithmetic  16.1 us (3%)
  between operations  13.8 us (3%)
    reduce_scatter x1, waiting for transfers between devices, per_device(): lax.psum_scatter(rounded.astype(jnp.float32).astype(jnp.bfloat16), 'shard...  203 us
    all_gather x1, waiting for transfers between devices, per_device(): lax.all_gather(dequantize(weight_values, weight_scales), 'shard', axis=0,...  99.2 us
    all_gather x1, waiting for transfers between devices, per_device(): lax.all_gather(group_part, 'replica')  92.5 us
    dot_general x1, matrix products, per_device(): grad_moved = jnp.dot(grad_pre, weight, preferred_element_type=jnp.float32)  23.9 us
    dot_general x1, matrix products, per_device(): lax.dot_general(grad_pre, moved, (((0,), (0,)), ((), ())), preferred_elem...  23.2 us
    dot_general x1, matrix products, per_device(): jnp.einsum('td,fd->tf', moved, weight, preferred_element_type=jnp.float32)  18.7 us
  transfers between devices with their start and end apart: 3, of which 3 were waited for; matrix products, arithmetic and copies ran while one was open for 6% of the time, Pallas kernels for 0%

profile of v2, /device:TPU:0, one launch (start us, length us, event | category | flops | bytes accessed | tf_op | source)
XLA Modules:
  0.0 493.1 jit_solution(1850491081331699919)
XLA Ops:
  7.2 0.0 copy-start
  7.2 0.0 copy-start.1
  7.2 0.0 copy-start.2
  7.2 0.0 all-gather.4.cloned.1.call-start
  7.2 1.0 copy.11
  8.2 0.7 mul.124
  8.9 3.1 fusion.18
  12.0 0.0 all-gather.4.cloned.1.call-update
  12.0 0.0 reduce-scatter.2.cloned.1.call-start
  12.1 0.0 copy-done
  12.1 0.3 convert_reduce_fusion
  12.4 0.7 fusion.15
  13.1 0.0 copy-done.1
  13.1 0.0 copy-done.2
  13.1 0.4 fusion.19
  13.6 2.5 fusion.17
  16.1 99.2 %all-gather.4.cloned.1.call-done = bf16[4864,1920]{1,0:T(8,128)(2,1)} async-done(((bf16[304,1920]{1,0:T(8,128)(2,1)}), bf16[4864,1920]{1,0:T(8,128)(2,1)}) %all-gather.4.cloned.1.call-update) | async-done | bytes 18677776 | tf_op jit(solution)/shard_map/all_gather | solution.py:64
  115.3 18.7 %multiply_convert_fusion = (bf16[512,4864]{1,0:T(8,128)(2,1)}, f32[512,4864]{1,0:T(8,128)}) fusion(bf16[512,1920]{1,0:T(8,128)(2,1)} %fusion.17, bf16[4864,1920]{1,0:T(8,128)(2,1)} %all-gather.4.cloned.1.call-done), kind=kOutput, calls=%fused_computation.10 | convolution fusion | flops 9585426432 | bytes 35586048 | tf_op jit(solution)/shard_map/td,fd->tf/dot_general | solution.py:65
  134.0 23.2 %convolution_convert_fusion = bf16[4864,1920]{1,0:T(8,128)(2,1)} fusion(bf16[512,1920]{1,0:T(8,128)(2,1)} %fusion.17, f32[512,4864]{1,0:T(8,128)} %get-tuple-element.8, bf16[512,4864]{1,0:T(8,128)(2,1)} %param.11), kind=kOutput, calls=%fused_computation | convolution fusion | flops 9622159360 | bytes 35586048 | tf_op jit(solution)/shard_map/dot_general | solution.py:70
  157.2 0.0 reduce-scatter.2.cloned.1.call-update
  157.2 0.0 all-gather.6.cloned.1.call-start
  157.3 203.4 %reduce-scatter.2.cloned.1.call-done = bf16[304,1920]{1,0:T(8,128)(2,1)} async-done(((bf16[4864,1920]{1,0:T(8,128)(2,1)}), bf16[304,1920]{1,0:T(8,128)(2,1)}) %reduce-scatter.2.cloned.1.call-update) | async-done | bytes 1167376 | tf_op jit(solution)/shard_map/reduce_scatter | solution.py:74
  360.7 0.0 all-gather.6.cloned.1.call-update
  360.7 23.9 %fusion.29 = (f32[512]{0:T(512)S(1)}, f32[512]{0:T(512)S(1)}, f32[512,1920]{1,0:T(8,128)S(1)}) fusion(f32[512]{0:T(512)S(1)} %add_rsqrt_fusion, f32[512]{0:T(512)S(1)} %broadcast_multiply_fusion.2, bf16[512,1920]{1,0:T(8,128)(2,1)S(1)} %copy-done, f32[2,1920]{1,0:T(2,128)S(1)} %get-tuple-element.5, bf16[4864,1920]{1,0:T(8,128)(2,1)} %all-gather.4.cloned.1.call-done, ...), kind=kOutput, calls=%fused_computation.42 | convolution fusion | flops 9619701760 | bytes 39541760 | tf_op jit(solution)/shard_map/dot_general | solution.py:69
  384.6 2.4 fusion.14
  387.0 92.5 %all-gather.6.cloned.1.call-done = bf16[2432,1920]{1,0:T(8,128)(2,1)} async-done(((bf16[304,1920]{1,0:T(8,128)(2,1)}), bf16[2432,1920]{1,0:T(8,128)(2,1)}) %all-gather.6.cloned.1.call-update) | async-done | bytes 9338896 | tf_op jit(solution)/shard_map/all_gather | solution.py:77
  479.5 5.6 %reduce_sum.50 = bf16[304,1920]{1,0:T(8,128)(2,1)S(1)} reduce(bf16[8,304,1920]{2,1,0:T(8,128)(2,1)} %bitcast.38, bf16[]{:T(256)} %constant.22.clone.1), dimensions={0}, to_apply=%region_3.0 | reduce | flops 4085760 | bytes 10506242 | tf_op jit(solution)/shard_map/reduce_sum | solution.py:77
  485.1 1.5 convert_element_type.47
  (4 shorter events, 0.0 us)
Async XLA Ops:
  7.2 4.9 %copy-start = (bf16[512,1920]{1,0:T(8,128)(2,1)S(1)}, bf16[512,1920]{1,0:T(8,128)(2,1)}, u32[]{:S(2)}) copy-start(bf16[512,1920]{1,0:T(8,128)(2,1)} %param.6) | copy-start | bytes 5898244
  7.2 5.9 %copy-start.1 = (f32[64,2,1920]{2,1,0:T(2,128)S(1)}, f32[64,2,1920]{2,1,0:T(2,128)}, u32[]{:S(2)}) copy-start(f32[64,2,1920]{2,1,0:T(2,128)} %param.8) | copy-start | bytes 2949124
  7.2 5.9 %copy-start.2 = (s32[2]{0:T(128)S(1)}, s32[2]{0:T(128)}, u32[]{:S(2)}) copy-start(s32[2]{0:T(128)} %param.7) | copy-start | bytes 28
  7.2 108.1 %all-gather.4.cloned.1.call-start = ((), (), s32[]{:S(2)}) async-start(), calls=%async_computation.1 | async-start | bytes 19845120 | tf_op jit(solution)/shard_map/all_gather | solution.py:64
  12.0 348.6 %reduce-scatter.2.cloned.1.call-start = ((), (), s32[]{:S(2)}) async-start(), calls=%async_computation.2 | async-start | bytes 19845120 | tf_op jit(solution)/shard_map/reduce_scatter | solution.py:74
  157.2 322.2 %all-gather.6.cloned.1.call-start = ((), (), s32[]{:S(2)}) async-start(), calls=%async_computation.3 | async-start | bytes 10506240 | tf_op jit(solution)/shard_map/all_gather | solution.py:77
Sparse Core Ops, SparseCore 0:
  12.2 103.0 all-gather.3
  157.4 203.2 reduce-scatter.1
  363.3 116.1 all-gather.5
